TPU v7x, 32 devices: a whole 2x2x4 slice. The times are simulated.
32 devices in a mesh: stream: 2 (over y), span: 4 (over z), wall: 4 (over x, core).
Axes of the slice: x: 2, y: 2, z: 4, core: 2. Of those that a mesh axis runs over, the one named last changes fastest.
Arguments:
- temp_in: float32 [8, 8, 8, 4096], P(None, None, None, ('stream', 'span', 'wall')), may hold values from -20 to 20
- velocity: bfloat16 [3, 8, 8, 8, 4096], P(None, None, None, None, ('stream', 'span', 'wall')), may hold values from -192 to 192
- spacing: float32 [3, 4096], P(None, ('stream', 'span', 'wall')), may hold values from 0.7 to 1.4
- conduct: float32 [4096], P(('stream', 'span', 'wall')), may hold values from 0.5 to 2
- shell_map: int32 [8, 8, 8, 32], P(None, None, 'stream', 'span'), may hold values from 0 to 4095, as said below
- shell_cond: float32 [16, 2048], P('stream', ('span', 'wall')), may hold values from 0.25 to 1
- shell_diag: float32 [16, 2048], P('stream', ('span', 'wall')), may hold values from 0.2 to 2
Outputs:
- temp_out: float32 [8, 8, 8, 4096], P(None, None, None, ('stream', 'span', 'wall'))
- shell_temp: float32 [16, 2048], P('stream', ('span', 'wall'))
- shell_resid: float32 [16, 2048], P('stream', ('span', 'wall'))
Inputs may be any that keep to these rules, and one draw needn't show every extreme that they name: `shell_map`: among the wall points of one block of 4 x 8 wall faces that share a streamwise and a spanwise slab, at most 1024 name the same owner t // 1024, and exactly 1024 name one owner.
All inputs are finite; a program needn't handle non-finite values.
Results may differ from a plain program's by a relative error of at most 0.0003.
Values sent between devices are 32-bit elements; how exact they have to be, the bound alone decides.
A program may use at most 128 MiB of HBM per device.

v0:
```python
import functools

import jax
import jax.numpy as jnp
import numpy as np
from jax import lax
from jax.experimental import pallas as pl
from jax.experimental.pallas import tpu as pltpu
from jax.sharding import PartitionSpec as P

SUBSTEPS = 2
TIME_STEP = 3e-05
MESH = pl.DeviceIdType.MESH
OFFSETS = [
    (x, y, z) for x in (-1, 0, 1) for y in (-1, 0, 1) for z in (-1, 0, 1) if (x, y, z) != (0, 0, 0)
]
AROUND = [(r, c) for r in (-1, 0, 1) for c in (-1, 0, 1) if (r, c) != (0, 0)]


def face_layout(counts):
    rows, start, total = {}, {}, 0
    for offset in OFFSETS:
        free = sum(1 for d in offset if d == 0)
        rows[offset] = 64 // sum(c for c, d in zip(counts, offset) if d) if free == 2 else 8
        start[offset] = total
        total += rows[offset]
    return rows, start, total


def gll_tables():
    degree = 7
    points = np.array(
        [
            -1.0,
            -0.8717401485096066,
            -0.5917001814331423,
            -0.2092992179024789,
            0.2092992179024789,
            0.5917001814331423,
            0.8717401485096066,
            1.0,
        ]
    )
    previous = np.ones(8)
    current = points.copy()
    for order in range(1, degree):
        following = ((2 * order + 1) * points * current - order * previous) / (order + 1)
        previous = current
        current = following
    weights = 2.0 / (degree * (degree + 1) * current * current)
    differ = points[:, None] - points[None, :]
    safe_differ = np.where(differ == 0.0, 1.0, differ)
    matrix = np.where(differ == 0.0, 0.0, current[:, None] / (current[None, :] * safe_differ))
    matrix[0, 0] = -degree * (degree + 1) / 4.0
    matrix[degree, degree] = degree * (degree + 1) / 4.0
    return weights, matrix


WEIGHTS, MATRIX = gll_tables()
STIFF = (MATRIX.T * WEIGHTS[None, :]) @ MATRIX / WEIGHTS[:, None]


def mxu_tables():
    parts = []
    eye4, eye8, eye32 = np.eye(4), np.eye(8), np.eye(32)
    for table in (MATRIX, STIFF):
        parts.append(np.kron(eye4, np.kron(table, eye8)))
    for table in (MATRIX, STIFF):
        parts.append(np.kron(eye32, table))
    whole = np.concatenate(parts, axis=0).astype(np.float32)
    high = whole.astype(jnp.bfloat16)
    low = (whole - high.astype(np.float32)).astype(jnp.bfloat16)
    return np.concatenate([high, high, low], axis=1)


def side(d):
    return 7 if d > 0 else 0


def roll(value, shift, axis):
    size = value.shape[axis]
    shift = shift % size
    return value if shift == 0 else pltpu.roll(value, shift, axis)


def kernel(
    dims,
    temp_hbm, vel_hbm, lhs_hbm, spacing_hbm, conduct_hbm, map_hbm, cond_hbm, diag_hbm,
    out_temp, out_shell, out_resid,
    temp_ref, vel, LHS, spacing_ref, conduct_ref, map_ref, cond_ref, diag_ref,
    T0, T, R, MASS, INVA,
    send0, recv0, send1, recv1, send2, recv2,
    gsend, flux_buf, Bt, Am, stat_send, stat_buf, z_send, z_buf, sum_send, sum_buf,
    face_ssem, face_rsem, gs_sem, gr_sem, st_ssem, st_rsem, z_ssem, z_rsem, p_ssem, p_rsem, loc_sem,
):
    NS, NP, NW, EX, EY, EZ = dims
    N = NS * NP * NW
    SX, SY = cond_ref.shape
    lanes = EX * EY * EZ
    s = lax.axis_index("stream")
    p = lax.axis_index("span")
    w = lax.axis_index("wall")
    me = (s * NP + p) * NW + w
    f32 = jnp.float32

    rows_of, START, _ = face_layout((EX, EY, EZ))

    def wrapped(index, size):
        return [index] + [
            jnp.where(index + d >= size, index + d - size, index + d) for d in range(1, size)
        ]

    s_of = wrapped(s, NS) if NS <= 4 else None
    p_of, w_of = wrapped(p, NP), wrapped(w, NW)
    s_up = jnp.where(s + 1 >= NS, 0, s + 1)
    s_down = jnp.where(s == 0, NS - 1, s - 1)
    s_near = (s, s_up, s_down)
    p_near = (p, p_of[1], p_of[NP - 1])
    w_near = (w, w_of[1], w_of[NW - 1])

    def everyone(visit):
        def plane(ds, s_there):
            for dp in reversed(range(NP)):
                for dw in reversed(range(NW)):
                    if isinstance(ds, int) and (ds, dp, dw) == (0, 0, 0):
                        continue
                    visit((ds * NP + dp) * NW + dw - 1, (s_there, p_of[dp], w_of[dw]))

        if s_of is not None:
            for ds in reversed(range(1, NS)):
                plane(ds, s_of[ds])
        else:
            def step(ds, _):
                plane(ds, jnp.where(s + ds >= NS, s + ds - NS, s + ds))
                return 0

            lax.fori_loop(1, NS, step, 0)
        plane(0, s)

    barrier = pltpu.get_barrier_semaphore()

    loads = [
        pltpu.make_async_copy(source, target, loc_sem.at[n])
        for n, (source, target) in enumerate(
            (
                (spacing_hbm, spacing_ref), (conduct_hbm, conduct_ref), (temp_hbm, temp_ref),
                (cond_hbm, cond_ref), (diag_hbm, diag_ref), (map_hbm, map_ref),
                (vel_hbm, vel), (lhs_hbm, LHS),
            )
        )
    ]
    for load_ in loads:
        load_.start()
    everyone(
        lambda slot, there: pl.semaphore_signal(
            barrier, inc=1, device_id=there, device_id_type=MESH
        )
    )
    lane = lax.broadcasted_iota(jnp.int32, (1, lanes), 1)
    la = lane // (EY * EZ)
    lb = lane // EZ % EY
    lc = lane % EZ
    sub = lax.broadcasted_iota(jnp.int32, (8, lanes), 0)

    def column(values):
        result = jnp.full((8, lanes), float(values[0]), f32)
        for k in range(1, 8):
            result = jnp.where(sub == k, float(values[k]), result)
        return result

    def exists(ds, dw):
        conds = []
        if ds:
            conds.append((s + ds >= 0) & (s + ds < NS))
        if dw:
            conds.append((w + dw >= 0) & (w + dw < NW))
        if not conds:
            return None
        return conds[0] if len(conds) == 1 else conds[0] & conds[1]

    def under(cond, body):
        if cond is None:
            body()
        else:
            pl.when(cond)(body)

    for load_ in loads[:3]:
        load_.wait()
    sp0, sp1, sp2 = spacing_ref[0:1, :], spacing_ref[1:2, :], spacing_ref[2:3, :]
    conduct = conduct_ref[...]
    sx, sy, sz = 2.0 / sp0, 2.0 / sp1, 2.0 / sp2
    wk = column(WEIGHTS)
    mass_kn = wk * (sp0 * sp1 * sp2 / 8.0)
    for i in range(8):
        for j in range(8):
            m = float(WEIGHTS[i] * WEIGHTS[j]) * mass_kn
            MASS[i, j] = m
            T0[1, i, j] = m
            T0[0, i, j] = m * temp_ref[i, j]
    def view(field, ch, offset):
        return tuple([ch] + [slice(None) if d == 0 else side(d) for d in offset])

    axes = ((la, EX, EY * EZ), (lb, EY, EZ), (lc, EZ, 1))

    def local_assemble(field, channels):
        for ch in range(channels):
            for axis, (step, place, count) in enumerate(
                ((EY * EZ, la, EX), (EZ, lb, EY), (1, lc, EZ))
            ):
                lo = [ch, slice(None), slice(None), slice(None)]
                hi = list(lo)
                lo[axis + 1], hi[axis + 1] = 0, 7
                lo, hi = tuple(lo), tuple(hi)
                f0 = field[lo].reshape(64, lanes)
                f7 = field[hi].reshape(64, lanes)
                n7 = f7 + jnp.where(place < count - 1, roll(f0, -step, 1), 0.0)
                n0 = f0 + jnp.where(place > 0, roll(f7, step, 1), 0.0)
                field[lo] = n0.reshape(8, 8, lanes)
                field[hi] = n7.reshape(8, 8, lanes)

    def descriptor(rnd, send, recv, index):
        offset = OFFSETS[index]
        rows = pl.ds(START[offset], rows_of[offset])
        return pltpu.make_async_remote_copy(
            src_ref=send.at[:, rows, :],
            dst_ref=recv.at[:, rows, :],
            send_sem=face_ssem.at[rnd, index],
            recv_sem=face_rsem.at[rnd, index],
            device_id=(s_near[offset[0]], p_near[offset[1]], w_near[offset[2]]),
            device_id_type=MESH,
        )

    order = sorted(range(len(OFFSETS)), key=lambda i: -sum(1 for d in OFFSETS[i] if d))

    groups_to = {}
    for index in order:
        groups_to.setdefault((OFFSETS[index][0], OFFSETS[index][2]), []).append(index)

    def send_faces(rnd, field, channels, send, recv):
        for index in order:
            offset = OFFSETS[index]
            n_rows = rows_of[offset]
            free = sum(1 for d in offset if d == 0)
            for ch in range(channels):
                if free == 0:
                    i, j, k = [side(d) for d in offset]
                    value = jnp.broadcast_to(field[ch, i, j, k : k + 1, :], (8, lanes))
                elif free == 1:
                    value = field[view(field, ch, offset)]
                else:
                    face = field[view(field, ch, offset)].reshape(64, lanes)
                    axis = [n for n in range(3) if offset[n]][0]
                    place, count, step = axes[axis]
                    own = count - 1 if offset[axis] > 0 else 0
                    value = roll(face[0:n_rows], -own * step, 1)
                    for g in range(1, count):
                        piece = roll(face[g * n_rows : (g + 1) * n_rows], (g - own) * step, 1)
                        value = jnp.where(place == g, piece, value)
                send[ch, START[offset] : START[offset] + n_rows, :] = value
        if rnd == 0:
            pl.semaphore_wait(barrier, N - 1)
        for (ds, dw), indices in groups_to.items():
            def body(indices=indices):
                for index in indices:
                    descriptor(rnd, send, recv, index).start()

            under(exists(ds, dw), body)

    def take_faces(rnd, field, channels, send, recv):
        for (ds, dw), indices in groups_to.items():
            def body(indices=indices):
                for index in indices:
                    descriptor(rnd, send, recv, index).wait_recv()

            under(exists(-ds, -dw), body)
        for index in reversed(order):
            offset = OFFSETS[index]
            n_rows = rows_of[offset]
            free = sum(1 for d in offset if d == 0)
            back = tuple(-d for d in offset)
            shift = 0
            mask = None
            for d, (place, count, step) in zip(offset, axes):
                if d:
                    shift -= d * (count - 1) * step
                    here = place == (0 if d > 0 else count - 1)
                    mask = here if mask is None else mask & here
            there = exists(back[0], back[2])
            if there is not None:
                mask = mask & there
            start = START[offset]
            for ch in range(channels):
                value = recv[ch, start : start + n_rows, :]
                if free == 2:
                    axis = [n for n in range(3) if back[n]][0]
                    place, count, step = axes[axis]
                    own = count - 1 if back[axis] > 0 else 0
                    value = jnp.concatenate(
                        [roll(value, (own - g) * step, 1) for g in range(count)], axis=0
                    )
                else:
                    value = roll(value, shift, 1)
                value = jnp.where(mask, value, 0.0)
                if free == 0:
                    i, j, k = [side(d) for d in back]
                    field[ch, i, j, k : k + 1, :] = field[ch, i, j, k : k + 1, :] + value[0:1]
                else:
                    spot = view(field, ch, back)
                    old = field[spot]
                    field[spot] = old + value.reshape(old.shape)

    def drain_faces(rnd, send, recv):
        for index in order:
            offset = OFFSETS[index]

            def body(index=index):
                descriptor(rnd, send, recv, index).wait_send()

            under(exists(offset[0], offset[2]), body)

    local_assemble(T0, 2)
    for load_ in loads[3:6]:
        load_.wait()
    stat_send[0] = cond_ref[...]
    stat_send[1] = diag_ref[...]
    send_faces(0, T0, 2, send0, recv0)

    ring = NP * NW
    spot_c = p * NW + w
    ring_up = jnp.where(spot_c == ring - 1, 0, spot_c + 1)
    ring_down = jnp.where(spot_c == 0, ring - 1, spot_c - 1)
    q_at = {1: (ring_up // NW, ring_up % NW), 0: (p, w), -1: (ring_down // NW, ring_down % NW)}

    def patch_copy(send, buf, ssem, rsem, index):
        dr, dc = AROUND[index]
        slot = (1 - dr) * 3 + (1 - dc)
        return pltpu.make_async_remote_copy(
            src_ref=send,
            dst_ref=buf.at[slot],
            send_sem=ssem.at[index],
            recv_sem=rsem.at[index],
            device_id=(s_near[dr],) + q_at[dc],
            device_id_type=MESH,
        )

    def patches(what, send, buf, ssem, rsem):
        for index, (dr, dc) in enumerate(AROUND):
            def body(index=index):
                copy = patch_copy(send, buf, ssem, rsem, index)
                if what == "start":
                    copy.start()
                elif what == "recv":
                    copy.wait_recv()
                else:
                    copy.wait_send()

            under(exists(-dr if what == "recv" else dr, 0), body)

    patches("start", stat_send, stat_buf, st_ssem, st_rsem)
    for slot in range(9):
        dr = slot // 3 - 1
        if dr:
            @pl.when(jnp.logical_not(exists(dr, 0)))
            def _(slot=slot):
                stat_buf[slot] = jnp.ones((2, SX, SY), f32)
                z_buf[slot] = jnp.zeros((SX, SY), f32)
    stat_buf[4] = stat_send[...]

    groups = 64 // EZ
    s_dev = SX * SY

    def split(value, size):
        if size & (size - 1):
            return value // size, value % size
        return lax.shift_right_logical(value, size.bit_length() - 1), value & (size - 1)

    codes = []
    for a in range(EX):
        t = map_ref[:, :, a, :].reshape(64, EY)
        owner, node = split(t, s_dev)
        row, col = split(node, SY)
        codes += [jnp.where(owner == w, row, SX).astype(f32), col.astype(f32)]
    bi = lax.broadcasted_iota(jnp.int32, (EY, lanes), 0)
    spread = jnp.where(bi == lb, 1.0, 0.0).astype(jnp.bfloat16)
    spreads = jnp.dot(
        jnp.concatenate(codes, axis=0).astype(jnp.bfloat16), spread, preferred_element_type=f32
    )
    picked = []
    for part in range(2):
        full = spreads[part * 64 : (part + 1) * 64]
        for a in range(1, EX):
            full = jnp.where(
                la == a, spreads[(2 * a + part) * 64 : (2 * a + part + 1) * 64], full
            )
        packed = full[0:groups]
        for g in range(1, EZ):
            packed = jnp.where(lc == g, full[g * groups : (g + 1) * groups], packed)
        picked.append(packed)
    qi = lax.broadcasted_iota(jnp.int32, (SY, lanes), 0).astype(f32)
    ri = lax.broadcasted_iota(jnp.int32, (SX, lanes), 0).astype(f32)
    for g in range(groups):
        row, col = picked[0][g : g + 1], picked[1][g : g + 1]
        Bt[g * lanes : (g + 1) * lanes, :] = jnp.where(qi == col, 1.0, 0.0).T.astype(jnp.bfloat16)
        Am[:, g * lanes : (g + 1) * lanes] = jnp.where(ri == row, 1.0, 0.0)

    keep_lane = jnp.where((lc == 0) & (w == 0), 0.0, 1.0)
    keep = jnp.where(sub == 0, jnp.broadcast_to(keep_lane, (8, lanes)), 1.0)

    take_faces(0, T0, 2, send0, recv0)
    for i in range(8):
        inv = keep / T0[1, i]
        T[0, i] = T0[0, i] * inv
        INVA[i] = inv * TIME_STEP
    for load_ in loads[6:]:
        load_.wait()

    cxx, cyy, czz = conduct * sx, conduct * sy, conduct * sz
    for rnd in range(1, SUBSTEPS + 1):
        send, recv = (send1, recv1) if rnd == 1 else (send2, recv2)
        def terms(get, top, bottom):
            value = jnp.concatenate(
                [jnp.concatenate([get(4 * h + q) for q in range(4)], axis=0) for h in range(2)],
                axis=1,
            )
            high = value.astype(jnp.bfloat16)
            low = (value - high.astype(f32)).astype(jnp.bfloat16)
            rhs = jnp.concatenate([high, low, high], axis=0)
            return jnp.dot(LHS[top:bottom, :], rhs, preferred_element_type=f32)

        def piece(found, kind, at):
            rows = kind * 256 + (at % 4) * 64
            cols = (at // 4) * lanes
            return found[rows : rows + 64, cols : cols + lanes].reshape(8, 8, lanes)

        along = terms(lambda j: T[0, :, j].reshape(64, lanes), 0, 512)
        for j in range(8):
            grad, stiff = piece(along, 0, j), piece(along, 1, j)
            R[0, :, j] = sx * (vel[0, :, j].astype(f32) * grad + cxx * stiff)
        across = terms(lambda i: T[0, i].reshape(64, lanes), 0, 1024)
        for i in range(8):
            total = R[0, i]
            total = total + sy * (
                vel[1, i].astype(f32) * piece(across, 0, i) + cyy * piece(across, 1, i)
            )
            total = total + sz * (
                vel[2, i].astype(f32) * piece(across, 2, i) + czz * piece(across, 3, i)
            )
            R[0, i] = -(MASS[i] * total)
        local_assemble(R, 1)
        send_faces(rnd, R, 1, send, recv)
        take_faces(rnd, R, 1, send, recv)
        for a in range(8):
            T[0, a] = keep * T[0, a] + R[0, a] * INVA[a]

    @pl.when(w == 0)
    def _():
        normal = float(MATRIX[0, 0]) * T[0, :, :, 0, :]
        for m in range(1, 8):
            normal = normal + float(MATRIX[0, m]) * T[0, :, :, m, :]
        area = conduct * sz * (sp0 * sp1 / 4.0)
        flux = jnp.concatenate(
            [normal[i] * (float(WEIGHTS[i]) * wk * area) for i in range(8)], axis=0
        )
        flux = jnp.where(lc == 0, flux, 0.0)
        packed = flux[0:groups]
        for g in range(1, EZ):
            packed = packed + roll(flux[g * groups : (g + 1) * groups], g, 1)
        gsend[...] = packed
        flux_buf[...] = packed

    def flux_copy(target):
        return pltpu.make_async_remote_copy(
            src_ref=gsend,
            dst_ref=flux_buf,
            send_sem=gs_sem.at[target],
            recv_sem=gr_sem.at[0],
            device_id=(s, p, target),
            device_id_type=MESH,
        )

    @pl.when(w == 0)
    def _():
        for target in range(1, NW):
            flux_copy(target).start()

    patches("recv", stat_send, stat_buf, st_ssem, st_rsem)

    def wide(get):
        return jnp.concatenate(
            [jnp.concatenate([get(3 * r + c) for c in range(3)], axis=1) for r in range(3)], axis=0
        )

    cond = wide(lambda slot: stat_buf[slot, 0])
    diag = wide(lambda slot: stat_buf[slot, 1])
    grow = s * SX - SX + lax.broadcasted_iota(jnp.int32, cond.shape, 0)
    cup = jnp.where(grow != NS * SX - 1, 0.5 * (cond + roll(cond, -1, 0)), 0.0)
    cdown = jnp.where(grow != 0, 0.5 * (cond + roll(cond, 1, 0)), 0.0)
    cright = 0.5 * (cond + roll(cond, -1, 1))
    cleft = 0.5 * (cond + roll(cond, 1, 1))
    jacobi = diag + cup + cdown + cright + cleft
    inv_jacobi = 1.0 / jacobi

    def apply(v):
        return (
            jacobi * v
            - cup * roll(v, -1, 0)
            - cdown * roll(v, 1, 0)
            - cright * roll(v, -1, 1)
            - cleft * roll(v, 1, 1)
        )

    def centre(v):
        return v[SX : 2 * SX, SY : 2 * SY]

    @pl.when(w != 0)
    def _():
        flux_copy(0).wait_recv()

    lhs = Am[...] * jnp.concatenate(
        [jnp.broadcast_to(flux_buf[g : g + 1, :], (SX, lanes)) for g in range(groups)], axis=1
    )
    high = lhs.astype(jnp.bfloat16).astype(f32)
    left = lhs - high
    middle = left.astype(jnp.bfloat16).astype(f32)
    parts = jnp.concatenate([high, middle, left - middle], axis=0).astype(jnp.bfloat16)
    found = jnp.dot(parts, Bt[...], preferred_element_type=f32)
    load = found[0:SX] + found[SX : 2 * SX] + found[2 * SX : 3 * SX]
    z_mine = load * centre(inv_jacobi)
    z_send[...] = z_mine
    patches("start", z_send, z_buf, z_ssem, z_rsem)
    z_buf[4] = z_mine
    for a in range(8):
        out_temp[a] = T[0, a]
    patches("recv", z_send, z_buf, z_ssem, z_rsem)
    z_wide = wide(lambda slot: z_buf[slot])
    image_wide = apply(z_wide)
    y_wide = image_wide * inv_jacobi
    ay = centre(apply(y_wide))
    image = centre(image_wide)
    y = centre(y_wide)

    def rowsum(v):
        return jnp.sum(v, axis=0, keepdims=True)

    fourth = SY // 4
    line = lax.broadcasted_iota(jnp.int32, (1, SY), 1) // fourth

    def folded(v):
        v = rowsum(v)
        v = v + roll(v, SY // 2, 1)
        return v + roll(v, SY // 4, 1)

    mine = folded(load * z_mine)
    for place, product in enumerate((z_mine * image, image * y, y * ay)):
        mine = jnp.where(line == place + 1, folded(product), mine)
    sum_send[...] = mine
    sum_buf[N - 1 : N, :] = mine

    def sum_copy(slot, there):
        return pltpu.make_async_remote_copy(
            src_ref=sum_send,
            dst_ref=sum_buf.at[pl.ds(slot, 1), :],
            send_sem=p_ssem.at[0],
            recv_sem=p_rsem.at[0],
            device_id=there,
            device_id_type=MESH,
        )

    everyone(lambda slot, there: sum_copy(slot, there).start())

    for rnd, (send, recv) in enumerate(((send0, recv0), (send1, recv1), (send2, recv2))):
        drain_faces(rnd, send, recv)
    patches("send", stat_send, stat_buf, st_ssem, st_rsem)
    patches("send", z_send, z_buf, z_ssem, z_rsem)

    @pl.when(w == 0)
    def _():
        for target in range(1, NW):
            flux_copy(target).wait_send()

    arrived = sum_buf.at[pl.ds(0, N - 1), :]
    pltpu.make_async_copy(arrived, arrived, p_ssem.at[0]).wait()
    pltpu.make_async_copy(arrived, arrived, p_rsem.at[0]).wait()
    totals = jnp.sum(sum_buf[...], axis=0, keepdims=True)
    rz, curve, m, q = [
        jnp.sum(jnp.where(line == place, totals, 0.0), axis=1, keepdims=True) for place in range(4)
    ]
    alpha = rz / curve
    new = alpha * alpha * m - rz
    beta = new / rz
    one = 1.0 + beta
    curve_next = one * one * curve - 2.0 * one * alpha * m + alpha * alpha * q
    alpha_next = new / curve_next
    direction = one * z_mine - alpha * y
    out_shell[...] = alpha * z_mine + alpha_next * direction
    out_resid[...] = load - alpha * image - alpha_next * (one * image - alpha * ay)


def hand_over(a_ref, b_ref, c_ref, x_ref, y_ref, z_ref):
    x_ref[...] = a_ref[...]
    y_ref[...] = b_ref[...]
    z_ref[...] = c_ref[...]


def per_device(sizes, temp_in, velocity, spacing, conduct, shell_map, shell_cond, shell_diag):
    NS, NP, NW = sizes
    N = NS * NP * NW
    lanes = temp_in.shape[3]
    EX, EY = shell_map.shape[2:]
    EZ = lanes // (EX * EY)
    groups = 64 // EZ
    SX, SY = shell_cond.shape
    ROWS = face_layout((EX, EY, EZ))[2]
    lhs = jnp.asarray(mxu_tables())
    f32 = jnp.float32
    block = (8, 8, 8, lanes)
    vmem = pl.BlockSpec(memory_space=pltpu.VMEM)
    V = pltpu.VMEM
    dma = pltpu.SemaphoreType.DMA
    outs = pl.pallas_call(
        functools.partial(kernel, (NS, NP, NW, EX, EY, EZ)),
        out_shape=(
            pltpu.VMEM(block, f32),
            pltpu.VMEM((SX, SY), f32),
            pltpu.VMEM((SX, SY), f32),
        ),
        in_specs=[pl.BlockSpec(memory_space=pltpu.HBM)] * 8,
        out_specs=(vmem, vmem, vmem),
        scratch_shapes=[
            V(block, f32), V((3,) + block, jnp.bfloat16), V(lhs.shape, jnp.bfloat16),
            V((3, lanes), f32), V((1, lanes), f32), V(shell_map.shape, jnp.int32),
            V((SX, SY), f32), V((SX, SY), f32),
            V((2,) + block, f32), V((1,) + block, f32), V((1,) + block, f32),
            V(block, f32), V(block, f32),
            V((2, ROWS, lanes), f32), V((2, ROWS, lanes), f32),
            V((1, ROWS, lanes), f32), V((1, ROWS, lanes), f32),
            V((1, ROWS, lanes), f32), V((1, ROWS, lanes), f32),
            V((groups, lanes), f32), V((groups, lanes), f32),
            V((groups * lanes, SY), jnp.bfloat16), V((SX, groups * lanes), f32),
            V((2, SX, SY), f32), V((9, 2, SX, SY), f32),
            V((SX, SY), f32), V((9, SX, SY), f32),
            V((1, SY), f32), V((N, SY), f32),
            dma((3, len(OFFSETS))), dma((3, len(OFFSETS))), dma((NW,)), dma((1,)),
            dma((8,)), dma((8,)), dma((8,)), dma((8,)), dma((1,)), dma((1,)), dma((8,)),
        ],
        compiler_params=pltpu.CompilerParams(
            collective_id=0, has_side_effects=True, vmem_limit_bytes=24 << 20
        ),
    )(
        *[
            pltpu.with_memory_space_constraint(x, pltpu.HBM)
            for x in (
                temp_in, velocity, lhs, spacing, conduct.reshape(1, lanes), shell_map, shell_cond,
                shell_diag,
            )
        ]
    )
    return pl.pallas_call(
        hand_over,
        out_shape=tuple(jax.ShapeDtypeStruct(o.shape, o.dtype) for o in outs),
        in_specs=[vmem] * 3,
        out_specs=(vmem,) * 3,
        compiler_params=pltpu.CompilerParams(vmem_limit_bytes=4 << 20),
    )(*outs)


def solution(mesh):
    sizes = (mesh.shape["stream"], mesh.shape["span"], mesh.shape["wall"])
    return jax.shard_map(
        functools.partial(per_device, sizes),
        mesh=mesh,
        in_specs=(
            P(None, None, None, ("stream", "span", "wall")),
            P(None, None, None, None, ("stream", "span", "wall")),
            P(None, ("stream", "span", "wall")),
            P(("stream", "span", "wall")),
            P(None, None, "stream", "span"),
            P("stream", ("span", "wall")),
            P("stream", ("span", "wall")),
        ),
        out_specs=(
            P(None, None, None, ("stream", "span", "wall")),
            P("stream", ("span", "wall")),
            P("stream", ("span", "wall")),
        ),
        check_vma=False,
    )
```

profile of v0, /device:TPU:0, one launch (start us, length us, event | category | flops | bytes accessed | tf_op | source)
XLA Modules:
  0.0 37.6 jit_solution(18090565032055383420)
XLA Ops:
  0.6 36.2 %shard_map.103 = (f32[8,8,8,128]{3,2,1,0:T(8,128)S(1)}, f32[8,128]{1,0:T(8,128)S(1)}, f32[8,128]{1,0:T(8,128)S(1)}) custom-call(f32[8,8,8,128]{3,2,1,0:T(8,128)} %temp_hbm.1, bf16[3,8,8,8,128]{4,3,2,1,0:T(8,128)(2,1)} %vel_hbm.1, bf16[1024,768]{1,0:T(8,128)(2,1)} %constant.2.clone.lhs_hbm, f32[3,128]{1,0:T(4,128)} %spacing_hbm.1, f32[1,128]{1,0:T(1,128)} %bitcast.1, ...), custom_call_target="tpu_custom_call" | custom-call | tf_op jit(solution)/shard_map/pallas_call | solution.py:620
  36.8 0.7 %shard_map.104 = (f32[8,8,8,128]{3,2,1,0:T(8,128)}, f32[8,128]{1,0:T(8,128)}, f32[8,128]{1,0:T(8,128)}) custom-call(f32[8,8,8,128]{3,2,1,0:T(8,128)S(1)} %get-tuple-element.6.a_ref, f32[8,128]{1,0:T(8,128)S(1)} %get-tuple-element.7.b_ref, f32[8,128]{1,0:T(8,128)S(1)} %get-tuple-element.8.c_ref), custom_call_target="tpu_custom_call" | custom-call | tf_op jit(solution)/shard_map/pallas_call | solution.py:658
where the time goes:
time: 37.7 us; the launch traced here: 37.6 us
  Pallas kernels  36.9 us (98%)
  between operations  0.64 us (2%)
    pallas_call x1, Pallas kernels, per_device(): pl.pallas_call(functools.partial(kernel, (NS, NP, NW, EX, EY, EZ)), out_s...  36.2 us

commit v1 on v0

--- a/solution.py
+++ b/solution.py
@@ -90,8 +90,10 @@
     temp_ref, vel, LHS, spacing_ref, conduct_ref, map_ref, cond_ref, diag_ref,
     T0, T, R, MASS, INVA,
     send0, recv0, send1, recv1, send2, recv2,
-    gsend, flux_buf, Bt, Am, stat_send, stat_buf, z_send, z_buf, sum_send, sum_buf,
-    face_ssem, face_rsem, gs_sem, gr_sem, st_ssem, st_rsem, z_ssem, z_rsem, p_ssem, p_rsem, loc_sem,
+    part_send, edge_send, area_send, part_buf, edge_buf, area_buf,
+    Bt, Am, stat_send, stat_buf, sum_send, sum_buf,
+    face_ssem, face_rsem, part_ssem, part_rsem, edge_rsem, area_ssem, area_rsem,
+    st_ssem, st_rsem, p_ssem, p_rsem, loc_sem,
 ):
     NS, NP, NW, EX, EY, EZ = dims
     N = NS * NP * NW
@@ -318,68 +320,32 @@
 
             under(exists(offset[0], offset[2]), body)
 
-    local_assemble(T0, 2)
-    for load_ in loads[3:6]:
-        load_.wait()
-    stat_send[0] = cond_ref[...]
-    stat_send[1] = diag_ref[...]
-    send_faces(0, T0, 2, send0, recv0)
-
-    ring = NP * NW
-    spot_c = p * NW + w
-    ring_up = jnp.where(spot_c == ring - 1, 0, spot_c + 1)
-    ring_down = jnp.where(spot_c == 0, ring - 1, spot_c - 1)
-    q_at = {1: (ring_up // NW, ring_up % NW), 0: (p, w), -1: (ring_down // NW, ring_down % NW)}
-
-    def patch_copy(send, buf, ssem, rsem, index):
-        dr, dc = AROUND[index]
-        slot = (1 - dr) * 3 + (1 - dc)
-        return pltpu.make_async_remote_copy(
-            src_ref=send,
-            dst_ref=buf.at[slot],
-            send_sem=ssem.at[index],
-            recv_sem=rsem.at[index],
-            device_id=(s_near[dr],) + q_at[dc],
-            device_id_type=MESH,
-        )
-
-    def patches(what, send, buf, ssem, rsem):
-        for index, (dr, dc) in enumerate(AROUND):
-            def body(index=index):
-                copy = patch_copy(send, buf, ssem, rsem, index)
-                if what == "start":
-                    copy.start()
-                elif what == "recv":
-                    copy.wait_recv()
-                else:
-                    copy.wait_send()
-
-            under(exists(-dr if what == "recv" else dr, 0), body)
-
-    patches("start", stat_send, stat_buf, st_ssem, st_rsem)
-    for slot in range(9):
-        dr = slot // 3 - 1
-        if dr:
-            @pl.when(jnp.logical_not(exists(dr, 0)))
-            def _(slot=slot):
-                stat_buf[slot] = jnp.ones((2, SX, SY), f32)
-                z_buf[slot] = jnp.zeros((SX, SY), f32)
-    stat_buf[4] = stat_send[...]
-
     groups = 64 // EZ
     s_dev = SX * SY
+    half = groups // 2
+    owners = 3 * SX
+    reach = min(2, NS - 1)
+    near = min(1, reach)
+    edge = (w == 0) | (w == NW - 1)
+    toward = jnp.where(w == 0, -1, 1)
 
     def split(value, size):
         if size & (size - 1):
             return value // size, value % size
         return lax.shift_right_logical(value, size.bit_length() - 1), value & (size - 1)
+
+    local_assemble(T0, 2)
+    for load_ in loads[3:6]:
+        load_.wait()
+    stat_send[0:SX] = cond_ref[...]
+    stat_send[SX : 2 * SX] = diag_ref[...]
 
     codes = []
     for a in range(EX):
         t = map_ref[:, :, a, :].reshape(64, EY)
         owner, node = split(t, s_dev)
         row, col = split(node, SY)
-        codes += [jnp.where(owner == w, row, SX).astype(f32), col.astype(f32)]
+        codes += [(owner * SX + row).astype(f32), col.astype(f32)]
     bi = lax.broadcasted_iota(jnp.int32, (EY, lanes), 0)
     spread = jnp.where(bi == lb, 1.0, 0.0).astype(jnp.bfloat16)
     spreads = jnp.dot(
@@ -396,12 +362,148 @@
         for g in range(1, EZ):
             packed = jnp.where(lc == g, full[g * groups : (g + 1) * groups], packed)
         picked.append(packed)
-    qi = lax.broadcasted_iota(jnp.int32, (SY, lanes), 0).astype(f32)
-    ri = lax.broadcasted_iota(jnp.int32, (SX, lanes), 0).astype(f32)
-    for g in range(groups):
-        row, col = picked[0][g : g + 1], picked[1][g : g + 1]
-        Bt[g * lanes : (g + 1) * lanes, :] = jnp.where(qi == col, 1.0, 0.0).T.astype(jnp.bfloat16)
-        Am[:, g * lanes : (g + 1) * lanes] = jnp.where(ri == row, 1.0, 0.0)
+    stat_send[2 * SX : 2 * SX + groups] = picked[0] * float(SY) + picked[1]
+
+    area = jnp.where(lc == 0, conduct * sz * (sp0 * sp1 / 4.0), 0.0)
+    for step in range(EZ.bit_length() - 1):
+        area = area + roll(area, 1 << step, 1)
+    area_send[...] = jnp.broadcast_to(area, (8, lanes))
+
+    @pl.when(w == 0)
+    def _():
+        area_buf[near, 0] = area_send[...]
+
+
+    qi = lax.broadcasted_iota(jnp.int32, (SY, lanes), 0)
+    ri = lax.broadcasted_iota(jnp.int32, (owners, lanes), 0)
+
+    def scatter_table(band, kind, code):
+        code = code.astype(jnp.int32)
+        row, col = split(code, SY)
+        shift = SX - SX * w
+        if kind:
+            shift = shift + toward * (SX * NW)
+        row = row + shift
+        for g in range(groups):
+            at = slice((kind * groups + g) * lanes, (kind * groups + g + 1) * lanes)
+            Bt[band, :, at] = jnp.where(qi == col[g : g + 1], 1.0, 0.0).astype(jnp.bfloat16)
+            Am[band, :, at] = jnp.where(ri == row[g : g + 1], 1.0, 0.0)
+
+    scatter_table(near, 0, picked[0] * float(SY) + picked[1])
+
+    def receivers(visit, wanted):
+        for ds in range(-reach, reach + 1):
+            def body(ds=ds):
+                for there in range(NW):
+                    if there == 0:
+                        plan = [(0, 0), (-1, 1), (1, -1), (-2, 2)]
+                    elif there == NW - 1:
+                        plan = [(0, 0), (1, 1), (-1, -1), (2, 2)]
+                    else:
+                        plan = [(0, 0), (-1, -1), (1, 1)]
+                    for turn, (dp, place) in enumerate(plan):
+                        full = dp == 0 or (place == 1 and there in (0, NW - 1))
+                        if not wanted(full, ds) or (ds, dp, there) == (0, 0, 0):
+                            continue
+                        index = ((ds + reach) * NW + there) * 4 + turn
+                        visit(full, ds, place, (s - ds, p_of[(-dp) % NP], there), index)
+
+            under(exists(-ds, 0), body)
+
+    def part_copy(ds, place, there=None, index=0):
+        return pltpu.make_async_remote_copy(
+            src_ref=part_send, dst_ref=part_buf.at[ds + reach, place],
+            send_sem=part_ssem.at[index], recv_sem=part_rsem.at[ds + reach, place],
+            device_id=(s, p, 0) if there is None else there, device_id_type=MESH,
+        )
+
+    def edge_copy(ds, place, there=None, index=0):
+        return pltpu.make_async_remote_copy(
+            src_ref=edge_send, dst_ref=edge_buf.at[ds + reach, place + 1],
+            send_sem=part_ssem.at[index], recv_sem=edge_rsem.at[ds + reach, place + 1],
+            device_id=(s, p, 0) if there is None else there, device_id_type=MESH,
+        )
+
+    def area_copy(ds, place, there=None, index=0):
+        return pltpu.make_async_remote_copy(
+            src_ref=area_send, dst_ref=area_buf.at[ds + near, place],
+            send_sem=area_ssem.at[index], recv_sem=area_rsem.at[ds + near, place],
+            device_id=(s, p, 0) if there is None else there, device_id_type=MESH,
+        )
+
+    def send_parts(what):
+        def visit(full, ds, place, there, index):
+            copy = (part_copy if full else edge_copy)(ds, place, there, index)
+            copy.start() if what == "start" else copy.wait_send()
+
+        receivers(visit, lambda full, ds: True)
+
+    def send_areas(what):
+        def visit(full, ds, place, there, index):
+            copy = area_copy(ds, place, there, index)
+            copy.start() if what == "start" else copy.wait_send()
+
+        receivers(visit, lambda full, ds: full and abs(ds) <= near)
+
+    def take(copy_of, ds, places):
+        for place in places:
+            copy_of(ds, place).wait_recv()
+
+    def take_all(copy_of, bands, main, side, sides):
+        for ds in bands:
+            def body(ds=ds):
+                if ds:
+                    take(copy_of, ds, main)
+                else:
+                    pl.when(w != 0)(lambda: take(copy_of, ds, main))
+                pl.when(edge)(lambda: take(copy_of, ds, side))
+                if sides:
+                    pl.when(jnp.logical_not(edge))(lambda: take(copy_of, ds, sides))
+
+            under(exists(ds, 0), body)
+
+    send_faces(0, T0, 2, send0, recv0)
+
+    ring = NP * NW
+    spot_c = p * NW + w
+    ring_up = jnp.where(spot_c == ring - 1, 0, spot_c + 1)
+    ring_down = jnp.where(spot_c == 0, ring - 1, spot_c - 1)
+    q_at = {1: (ring_up // NW, ring_up % NW), 0: (p, w), -1: (ring_down // NW, ring_down % NW)}
+
+    def patch_copy(index):
+        dr, dc = AROUND[index]
+        slot = (1 - dr) * 3 + (1 - dc)
+        return pltpu.make_async_remote_copy(
+            src_ref=stat_send,
+            dst_ref=stat_buf.at[slot],
+            send_sem=st_ssem.at[index],
+            recv_sem=st_rsem.at[index],
+            device_id=(s_near[dr],) + q_at[dc],
+            device_id_type=MESH,
+        )
+
+    def patches(what):
+        for index, (dr, dc) in enumerate(AROUND):
+            def body(index=index):
+                copy = patch_copy(index)
+                if what == "start":
+                    copy.start()
+                elif what == "recv":
+                    copy.wait_recv()
+                else:
+                    copy.wait_send()
+
+            under(exists(-dr if what == "recv" else dr, 0), body)
+
+    patches("start")
+    pl.when(w == 0)(lambda: send_areas("start"))
+    for slot in range(9):
+        dr = slot // 3 - 1
+        if dr:
+            @pl.when(jnp.logical_not(exists(dr, 0)))
+            def _(slot=slot):
+                stat_buf[slot] = jnp.ones(stat_send.shape, f32)
+    stat_buf[4] = stat_send[...]
 
     keep_lane = jnp.where((lc == 0) & (w == 0), 0.0, 1.0)
     keep = jnp.where(sub == 0, jnp.broadcast_to(keep_lane, (8, lanes)), 1.0)
@@ -415,6 +517,43 @@
         load_.wait()
 
     cxx, cyy, czz = conduct * sx, conduct * sy, conduct * sz
+
+    def other_tables():
+        patches("recv")
+        for ds in range(-near, near + 1):
+            for kind in range(2):
+                if (ds, kind) == (0, 0):
+                    continue
+                slot = (ds + 1) * 3 + 1 + (toward if kind else 0)
+                scatter_table(ds + near, kind, stat_buf[slot, 2 * SX : 2 * SX + groups])
+
+    def wall_part():
+        shared = jnp.where((sub == 0) & (lb == 0), 0.5, 1.0)
+        shared = jnp.where((sub == 7) & (lb == EY - 1), 0.5, shared)
+        rows = []
+        for i in range(8):
+            mine = float(MATRIX[0, 1]) * T[0, i, :, 1, :]
+            rate = float(MATRIX[0, 1]) * (R[0, i, :, 1, :] * INVA[i, :, 1, :])
+            for m in range(2, 8):
+                mine = mine + float(MATRIX[0, m]) * T[0, i, :, m, :]
+                rate = rate + float(MATRIX[0, m]) * (R[0, i, :, m, :] * INVA[i, :, m, :])
+            weight = shared
+            if i == 0:
+                weight = jnp.where((la == 0) & (s > 0), 0.5 * shared, shared)
+            elif i == 7:
+                weight = jnp.where((la == EX - 1) & (s < NS - 1), 0.5 * shared, shared)
+            rows.append(jnp.where(lc == 0, mine * weight + rate, 0.0))
+        flat = jnp.concatenate(rows, axis=0)
+        packed = flat[0:groups]
+        for g in range(1, EZ):
+            packed = packed + roll(flat[g * groups : (g + 1) * groups], g, 1)
+        part_send[...] = packed
+        edge_send[...] = jnp.where(
+            (sub == 0) | (sub == 7), packed[0:half], roll(packed[half:groups], 2, 0)
+        )
+        part_buf[reach, 0] = packed
+        send_parts("start")
+
     for rnd in range(1, SUBSTEPS + 1):
         send, recv = (send1, recv1) if rnd == 1 else (send2, recv2)
         def terms(get, top, bottom):
@@ -447,51 +586,23 @@
             )
             R[0, i] = -(MASS[i] * total)
         local_assemble(R, 1)
+        if rnd == SUBSTEPS:
+            pl.when(w == 0)(lambda: wall_part())
         send_faces(rnd, R, 1, send, recv)
-        take_faces(rnd, R, 1, send, recv)
-        for a in range(8):
-            T[0, a] = keep * T[0, a] + R[0, a] * INVA[a]
-
-    @pl.when(w == 0)
-    def _():
-        normal = float(MATRIX[0, 0]) * T[0, :, :, 0, :]
-        for m in range(1, 8):
-            normal = normal + float(MATRIX[0, m]) * T[0, :, :, m, :]
-        area = conduct * sz * (sp0 * sp1 / 4.0)
-        flux = jnp.concatenate(
-            [normal[i] * (float(WEIGHTS[i]) * wk * area) for i in range(8)], axis=0
-        )
-        flux = jnp.where(lc == 0, flux, 0.0)
-        packed = flux[0:groups]
-        for g in range(1, EZ):
-            packed = packed + roll(flux[g * groups : (g + 1) * groups], g, 1)
-        gsend[...] = packed
-        flux_buf[...] = packed
-
-    def flux_copy(target):
-        return pltpu.make_async_remote_copy(
-            src_ref=gsend,
-            dst_ref=flux_buf,
-            send_sem=gs_sem.at[target],
-            recv_sem=gr_sem.at[0],
-            device_id=(s, p, target),
-            device_id_type=MESH,
-        )
-
-    @pl.when(w == 0)
-    def _():
-        for target in range(1, NW):
-            flux_copy(target).start()
-
-    patches("recv", stat_send, stat_buf, st_ssem, st_rsem)
+        if rnd < SUBSTEPS:
+            if rnd == 1:
+                other_tables()
+            take_faces(rnd, R, 1, send, recv)
+            for a in range(8):
+                T[0, a] = keep * T[0, a] + R[0, a] * INVA[a]
 
     def wide(get):
         return jnp.concatenate(
             [jnp.concatenate([get(3 * r + c) for c in range(3)], axis=1) for r in range(3)], axis=0
         )
 
-    cond = wide(lambda slot: stat_buf[slot, 0])
-    diag = wide(lambda slot: stat_buf[slot, 1])
+    cond = wide(lambda slot: stat_buf[slot, 0:SX])
+    diag = wide(lambda slot: stat_buf[slot, SX : 2 * SX])
     grow = s * SX - SX + lax.broadcasted_iota(jnp.int32, cond.shape, 0)
     cup = jnp.where(grow != NS * SX - 1, 0.5 * (cond + roll(cond, -1, 0)), 0.0)
     cdown = jnp.where(grow != 0, 0.5 * (cond + roll(cond, 1, 0)), 0.0)
@@ -512,27 +623,107 @@
     def centre(v):
         return v[SX : 2 * SX, SY : 2 * SY]
 
-    @pl.when(w != 0)
-    def _():
-        flux_copy(0).wait_recv()
-
-    lhs = Am[...] * jnp.concatenate(
-        [jnp.broadcast_to(flux_buf[g : g + 1, :], (SX, lanes)) for g in range(groups)], axis=1
-    )
-    high = lhs.astype(jnp.bfloat16).astype(f32)
-    left = lhs - high
-    middle = left.astype(jnp.bfloat16).astype(f32)
-    parts = jnp.concatenate([high, middle, left - middle], axis=0).astype(jnp.bfloat16)
-    found = jnp.dot(parts, Bt[...], preferred_element_type=f32)
-    load = found[0:SX] + found[SX : 2 * SX] + found[2 * SX : 3 * SX]
-    z_mine = load * centre(inv_jacobi)
-    z_send[...] = z_mine
-    patches("start", z_send, z_buf, z_ssem, z_rsem)
-    z_buf[4] = z_mine
-    for a in range(8):
-        out_temp[a] = T[0, a]
-    patches("recv", z_send, z_buf, z_ssem, z_rsem)
-    z_wide = wide(lambda slot: z_buf[slot])
+    point = lax.broadcasted_iota(jnp.int32, (groups, lanes), 0) + lc * groups
+    wi = jnp.full((groups, lanes), float(WEIGHTS[0]), f32)
+    wj = jnp.full((groups, lanes), float(WEIGHTS[0]), f32)
+    for k in range(1, 8):
+        wi = jnp.where(point // 8 == k, float(WEIGHTS[k]), wi)
+        wj = jnp.where(point % 8 == k, float(WEIGHTS[k]), wj)
+    wij = wi * wj
+
+    take_all(area_copy, range(-near, near + 1), (0,), (1,), ())
+    bands = range(-reach, reach + 1)
+    take_all(part_copy, bands, (0,), (1,), ())
+    take_all(edge_copy, bands, (), (-1, 2), (-1, 1))
+
+    def both(mask, cond):
+        return mask if cond is None else mask & cond
+
+    def edge_rows(part):
+        return jnp.where(
+            (sub == 0) | (sub == 7), part[0:half], roll(part[half:groups], 2, 0)
+        )
+
+    def span_sum(part, above, below):
+        above = roll(above, (EY - 1) * EZ, 1)
+        below = roll(below, -(EY - 1) * EZ, 1)
+        high = (sub == 7) & (lb == EY - 1)
+        low = (sub == 0) & (lb == 0)
+        rows = []
+        for h, (first, last) in enumerate(((0, 7), (2, 1))):
+            rows.append(
+                part[h * half : (h + 1) * half]
+                + jnp.where(high, above[first : first + 1], 0.0)
+                + jnp.where(low, below[last : last + 1], 0.0)
+            )
+        return rows
+
+    summed = {}
+    for ds in bands:
+        mains, sides = part_buf[ds + reach, 0], part_buf[ds + reach, 1]
+        back, ahead, far = [edge_buf[ds + reach, place + 1] for place in (-1, 1, 2)]
+        main_edge = edge_rows(mains)
+        ahead = jnp.where(edge, edge_rows(sides), ahead)
+        up = toward > 0
+        summed[ds, 0] = span_sum(mains, jnp.where(up, ahead, back), jnp.where(up, back, ahead))
+        summed[ds, 1] = span_sum(
+            sides, jnp.where(up, far, main_edge), jnp.where(up, main_edge, far)
+        )
+    jump = (EX - 1) * EY * EZ + EZ - 1
+    loads_wide = []
+    for ds in range(-1, 2):
+        if abs(ds) > near:
+            loads_wide.append(jnp.zeros((SX, owners * SY // SX), f32))
+            continue
+        here = exists(ds, 0)
+        lhs = []
+        for kind in range(2):
+            even, odd = summed[ds, kind]
+            if ds + 1 <= reach:
+                more = roll(summed[ds + 1, kind][0], jump, 1)
+                odd = odd + jnp.where(
+                    both((la == EX - 1) & (lc == EZ - 1), exists(ds + 1, 0)), more, 0.0
+                )
+            if ds - 1 >= -reach:
+                more = roll(summed[ds - 1, kind][1], -jump, 1)
+                even = even + jnp.where(both((la == 0) & (lc == 0), exists(ds - 1, 0)), more, 0.0)
+            scale = area_buf[ds + near, kind]
+            flux = jnp.concatenate([even * scale, odd * scale], axis=0) * wij
+            valid = edge if kind else None
+            if here is not None:
+                valid = here if valid is None else valid & here
+            if valid is not None:
+                flux = jnp.where(valid, flux, 0.0)
+            high = flux.astype(jnp.bfloat16).astype(f32)
+            for piece_ in (high, flux - high):
+                lhs.append(
+                    Am[ds + near, :, kind * groups * lanes : (kind + 1) * groups * lanes]
+                    * jnp.concatenate(
+                        [
+                            jnp.broadcast_to(piece_[g : g + 1], (owners, lanes))
+                            for g in range(groups)
+                        ],
+                        axis=1,
+                    )
+                )
+        lhs = jnp.concatenate(
+            [
+                jnp.concatenate([lhs[0], lhs[2]], axis=1),
+                jnp.concatenate([lhs[1], lhs[3]], axis=1),
+            ],
+            axis=0,
+        ).astype(jnp.bfloat16)
+        found = lax.dot_general(
+            lhs, Bt[ds + near], (((1,), (1,)), ((), ())), preferred_element_type=f32
+        )
+        found = found[0:owners] + found[owners : 2 * owners]
+        loads_wide.append(
+            jnp.concatenate([found[c * SX : (c + 1) * SX] for c in range(3)], axis=1)
+        )
+    load_wide = jnp.concatenate(loads_wide, axis=0)
+    load = centre(load_wide)
+    z_wide = load_wide * inv_jacobi
+    z_mine = centre(z_wide)
     image_wide = apply(z_wide)
     y_wide = image_wide * inv_jacobi
     ay = centre(apply(y_wide))
@@ -568,15 +759,18 @@
 
     everyone(lambda slot, there: sum_copy(slot, there).start())
 
+    take_faces(SUBSTEPS, R, 1, send2, recv2)
+    for a in range(8):
+        out_temp[a] = keep * T[0, a] + R[0, a] * INVA[a]
+
     for rnd, (send, recv) in enumerate(((send0, recv0), (send1, recv1), (send2, recv2))):
         drain_faces(rnd, send, recv)
-    patches("send", stat_send, stat_buf, st_ssem, st_rsem)
-    patches("send", z_send, z_buf, z_ssem, z_rsem)
+    patches("send")
 
     @pl.when(w == 0)
     def _():
-        for target in range(1, NW):
-            flux_copy(target).wait_send()
+        send_areas("send")
+        send_parts("send")
 
     arrived = sum_buf.at[pl.ds(0, N - 1), :]
     pltpu.make_async_copy(arrived, arrived, p_ssem.at[0]).wait()
@@ -609,7 +803,10 @@
     EX, EY = shell_map.shape[2:]
     EZ = lanes // (EX * EY)
     groups = 64 // EZ
+    reach = min(2, NS - 1)
+    near = min(1, reach)
     SX, SY = shell_cond.shape
+    assert lanes == SY and groups == 16 and NP > 2 and NW > 1
     ROWS = face_layout((EX, EY, EZ))[2]
     lhs = jnp.asarray(mxu_tables())
     f32 = jnp.float32
@@ -635,13 +832,17 @@
             V((2, ROWS, lanes), f32), V((2, ROWS, lanes), f32),
             V((1, ROWS, lanes), f32), V((1, ROWS, lanes), f32),
             V((1, ROWS, lanes), f32), V((1, ROWS, lanes), f32),
-            V((groups, lanes), f32), V((groups, lanes), f32),
-            V((groups * lanes, SY), jnp.bfloat16), V((SX, groups * lanes), f32),
-            V((2, SX, SY), f32), V((9, 2, SX, SY), f32),
-            V((SX, SY), f32), V((9, SX, SY), f32),
+            V((groups, lanes), f32), V((8, lanes), f32), V((8, lanes), f32),
+            V((2 * reach + 1, 2, groups, lanes), f32), V((2 * reach + 1, 4, 8, lanes), f32),
+            V((2 * near + 1, 2, 8, lanes), f32),
+            V((2 * near + 1, SY, 2 * groups * lanes), jnp.bfloat16),
+            V((2 * near + 1, 3 * SX, 2 * groups * lanes), f32),
+            V((2 * SX + groups, SY), f32), V((9, 2 * SX + groups, SY), f32),
             V((1, SY), f32), V((N, SY), f32),
-            dma((3, len(OFFSETS))), dma((3, len(OFFSETS))), dma((NW,)), dma((1,)),
-            dma((8,)), dma((8,)), dma((8,)), dma((8,)), dma((1,)), dma((1,)), dma((8,)),
+            dma((3, len(OFFSETS))), dma((3, len(OFFSETS))),
+            dma(((2 * reach + 1) * NW * 4,)), dma((2 * reach + 1, 2)), dma((2 * reach + 1, 4)),
+            dma(((2 * reach + 1) * NW * 4,)), dma((2 * near + 1, 2)),
+            dma((8,)), dma((8,)), dma((1,)), dma((1,)), dma((8,)),
         ],
         compiler_params=pltpu.CompilerParams(
             collective_id=0, has_side_effects=True, vmem_limit_bytes=24 << 20

time: 37.7 us -> 35.1 us (0.931)
  Pallas kernels: 36.9 us -> 34.3 us
    pallas_call x1, Pallas kernels: 36.2 us -> 33.6 us  [per_device(): pl.pallas_call(functools.partial(kernel, (NS, NP, NW, EX, EY, EZ)), out_s...]
where the time goes in v1:
time: 35.1 us; the launch traced here: 34.9 us
  Pallas kernels  34.3 us (98%)
  between operations  0.64 us (2%)
    pallas_call x1, Pallas kernels, per_device(): pl.pallas_call(functools.partial(kernel, (NS, NP, NW, EX, EY, EZ)), out_s...  33.6 us
    pallas_call x1, Pallas kernels, per_device(): pl.pallas_call(hand_over, out_shape=tuple((jax.ShapeDtypeStruct(o.shape,...  0.73 us

profile of v1, /device:TPU:0, one launch (start us, length us, event | category | flops | bytes accessed | tf_op | source)
XLA Modules:
  0.0 34.9 jit_solution(5542278132669357688)
XLA Ops:
  0.6 33.6 %shard_map.103 = (f32[8,8,8,128]{3,2,1,0:T(8,128)S(1)}, f32[8,128]{1,0:T(8,128)S(1)}, f32[8,128]{1,0:T(8,128)S(1)}) custom-call(f32[8,8,8,128]{3,2,1,0:T(8,128)} %temp_hbm.1, bf16[3,8,8,8,128]{4,3,2,1,0:T(8,128)(2,1)} %vel_hbm.1, bf16[1024,768]{1,0:T(8,128)(2,1)} %constant.2.clone.lhs_hbm, f32[3,128]{1,0:T(4,128)} %spacing_hbm.1, f32[1,128]{1,0:T(1,128)} %bitcast.1, ...), custom_call_target="tpu_custom_call" | custom-call | tf_op jit(solution)/shard_map/pallas_call | solution.py:817
  34.2 0.7 %shard_map.104 = (f32[8,8,8,128]{3,2,1,0:T(8,128)}, f32[8,128]{1,0:T(8,128)}, f32[8,128]{1,0:T(8,128)}) custom-call(f32[8,8,8,128]{3,2,1,0:T(8,128)S(1)} %get-tuple-element.6.a_ref, f32[8,128]{1,0:T(8,128)S(1)} %get-tuple-element.7.b_ref, f32[8,128]{1,0:T(8,128)S(1)} %get-tuple-element.8.c_ref), custom_call_target="tpu_custom_call" | custom-call | tf_op jit(solution)/shard_map/pallas_call | solution.py:859

commit v2 on v1

--- a/solution.py
+++ b/solution.py
@@ -91,7 +91,7 @@
     T0, T, R, MASS, INVA,
     send0, recv0, send1, recv1, send2, recv2,
     part_send, edge_send, area_send, part_buf, edge_buf, area_buf,
-    Bt, Am, stat_send, stat_buf, sum_send, sum_buf,
+    Bt, Am, Am_other, Side, stat_send, stat_buf, sum_send, sum_buf,
     face_ssem, face_rsem, part_ssem, part_rsem, edge_rsem, area_ssem, area_rsem,
     st_ssem, st_rsem, p_ssem, p_rsem, loc_sem,
 ):
@@ -376,20 +376,20 @@
 
     qi = lax.broadcasted_iota(jnp.int32, (SY, lanes), 0)
     ri = lax.broadcasted_iota(jnp.int32, (owners, lanes), 0)
-
-    def scatter_table(band, kind, code):
-        code = code.astype(jnp.int32)
-        row, col = split(code, SY)
-        shift = SX - SX * w
-        if kind:
-            shift = shift + toward * (SX * NW)
-        row = row + shift
+    others = [None] if NS == 2 else list(range(-1, 2, 2)) if NS > 2 else []
+
+    def row_side(sign):
+        return jnp.where(s == 0, 1, -1) if sign is None else sign
+
+    def scatter_table(code, slot, rows, target):
+        row, col = split(code.astype(jnp.int32), SY)
+        row = row + (SX - SX * w)
         for g in range(groups):
-            at = slice((kind * groups + g) * lanes, (kind * groups + g + 1) * lanes)
-            Bt[band, :, at] = jnp.where(qi == col[g : g + 1], 1.0, 0.0).astype(jnp.bfloat16)
-            Am[band, :, at] = jnp.where(ri == row[g : g + 1], 1.0, 0.0)
-
-    scatter_table(near, 0, picked[0] * float(SY) + picked[1])
+            at = slice(g * lanes, (g + 1) * lanes)
+            Bt[slot, :, at] = jnp.where(qi == col[g : g + 1], 1.0, 0.0).astype(jnp.bfloat16)
+            target[:, at] = jnp.where(rows == row[g : g + 1], 1.0, 0.0)
+
+    scatter_table(picked[0] * float(SY) + picked[1], 0, ri, Am)
 
     def receivers(visit, wanted):
         for ds in range(-reach, reach + 1):
@@ -518,31 +518,62 @@
 
     cxx, cyy, czz = conduct * sx, conduct * sy, conduct * sz
 
+    def side_table(code, slot):
+        code = code.astype(jnp.int32)
+        node = lax.broadcasted_iota(jnp.int32, (2 * SX, lanes), 0)
+        first = jnp.where(w == 0, (NW - 1) * s_dev + SY - 2, 0)
+        node = first + node % SX * SY + node // SX
+        for g in range(groups):
+            Side[slot, :, g * lanes : (g + 1) * lanes] = jnp.where(
+                node == code[g : g + 1], 1.0, 0.0
+            ).astype(jnp.bfloat16)
+
     def other_tables():
         patches("recv")
-        for ds in range(-near, near + 1):
-            for kind in range(2):
-                if (ds, kind) == (0, 0):
-                    continue
-                slot = (ds + 1) * 3 + 1 + (toward if kind else 0)
-                scatter_table(ds + near, kind, stat_buf[slot, 2 * SX : 2 * SX + groups])
+        side_table(stat_buf[4 + toward, 2 * SX : 2 * SX + groups], 0)
+        for n, sign in enumerate(others):
+            sign = row_side(sign)
+            slot = (sign + 1) * 3 + 1
+            ro = lax.broadcasted_iota(jnp.int32, (8, lanes), 0)
+            rows = ro // 2 * SX + ro % 2 + jnp.where(sign > 0, 0, SX - 2)
+            scatter_table(
+                stat_buf[slot, 2 * SX : 2 * SX + groups], n + 1, rows, Am_other.at[n]
+            )
+            side_table(stat_buf[slot + toward, 2 * SX : 2 * SX + groups], n + 1)
+
+    def fold(values):
+        for width in (4, 2, 1):
+            low = sub // width % 2 == 0
+            count = len(values) // 2
+            values = [
+                jnp.where(low, values[n], values[n + count])
+                + jnp.where(
+                    low,
+                    roll(values[n], -width, 0),
+                    roll(values[n + count], width, 0),
+                )
+                for n in range(count)
+            ]
+        return values[0]
+
+    normal_row = column(MATRIX[0])
 
     def wall_part():
-        shared = jnp.where((sub == 0) & (lb == 0), 0.5, 1.0)
-        shared = jnp.where((sub == 7) & (lb == EY - 1), 0.5, shared)
+        across_row = [normal_row] * 8
+        across_row[0] = jnp.where(lb == 0, 0.5 * normal_row, normal_row)
+        across_row[7] = jnp.where(lb == EY - 1, 0.5 * normal_row, normal_row)
         rows = []
         for i in range(8):
-            mine = float(MATRIX[0, 1]) * T[0, i, :, 1, :]
-            rate = float(MATRIX[0, 1]) * (R[0, i, :, 1, :] * INVA[i, :, 1, :])
-            for m in range(2, 8):
-                mine = mine + float(MATRIX[0, m]) * T[0, i, :, m, :]
-                rate = rate + float(MATRIX[0, m]) * (R[0, i, :, m, :] * INVA[i, :, m, :])
-            weight = shared
+            scale = None
             if i == 0:
-                weight = jnp.where((la == 0) & (s > 0), 0.5 * shared, shared)
+                scale = jnp.where((la == 0) & (s > 0), 0.5, 1.0)
             elif i == 7:
-                weight = jnp.where((la == EX - 1) & (s < NS - 1), 0.5 * shared, shared)
-            rows.append(jnp.where(lc == 0, mine * weight + rate, 0.0))
+                scale = jnp.where((la == EX - 1) & (s < NS - 1), 0.5, 1.0)
+            terms = []
+            for j in range(8):
+                weight = across_row[j] if scale is None else across_row[j] * scale
+                terms.append(T[0, i, j] * weight + R[0, i, j] * (INVA[i, j] * normal_row))
+            rows.append(jnp.where(lc == 0, fold(terms), 0.0))
         flat = jnp.concatenate(rows, axis=0)
         packed = flat[0:groups]
         for g in range(1, EZ):
@@ -658,69 +689,118 @@
             )
         return rows
 
-    summed = {}
-    for ds in bands:
+    def band_sum(ds):
         mains, sides = part_buf[ds + reach, 0], part_buf[ds + reach, 1]
         back, ahead, far = [edge_buf[ds + reach, place + 1] for place in (-1, 1, 2)]
         main_edge = edge_rows(mains)
         ahead = jnp.where(edge, edge_rows(sides), ahead)
         up = toward > 0
-        summed[ds, 0] = span_sum(mains, jnp.where(up, ahead, back), jnp.where(up, back, ahead))
-        summed[ds, 1] = span_sum(
-            sides, jnp.where(up, far, main_edge), jnp.where(up, main_edge, far)
-        )
+        return (
+            span_sum(mains, jnp.where(up, ahead, back), jnp.where(up, back, ahead)),
+            span_sum(sides, jnp.where(up, far, main_edge), jnp.where(up, main_edge, far)),
+        )
+
     jump = (EX - 1) * EY * EZ + EZ - 1
-    loads_wide = []
-    for ds in range(-1, 2):
-        if abs(ds) > near:
-            loads_wide.append(jnp.zeros((SX, owners * SY // SX), f32))
+    last = (la == EX - 1) & (lc == EZ - 1)
+    first = (la == 0) & (lc == 0)
+
+    def stream_sum(here, above, below):
+        even, odd = here
+        if above is not None:
+            odd = odd + jnp.where(both(last, above[1]), roll(above[0][0], jump, 1), 0.0)
+        if below is not None:
+            even = even + jnp.where(both(first, below[1]), roll(below[0][1], -jump, 1), 0.0)
+        return even, odd
+
+    def halves(pair, scale, valid):
+        flux = jnp.concatenate([pair[0] * scale, pair[1] * scale], axis=0) * wij
+        if valid is not None:
+            flux = jnp.where(valid, flux, 0.0)
+        high = flux.astype(jnp.bfloat16).astype(f32)
+        return high, flux - high
+
+    def spread_rows(v, count):
+        return jnp.concatenate(
+            [jnp.broadcast_to(v[g : g + 1], (count, lanes)) for g in range(groups)], axis=1
+        )
+
+    def contract(left, right):
+        return lax.dot_general(
+            left, right, (((1,), (1,)), ((), ())), preferred_element_type=f32
+        )
+
+    def main_load(parts, table, slot, count):
+        left = jnp.concatenate([table * spread_rows(v, count) for v in parts], axis=0)
+        out = contract(left.astype(jnp.bfloat16), Bt[slot])
+        return out[0:count] + out[count : 2 * count]
+
+    column_at = lax.broadcasted_iota(jnp.int32, (SX, SY), 1) - jnp.where(w == 0, SY - 2, 0)
+
+    def side_load(parts, slot):
+        right = jnp.concatenate([spread_rows(v, 8) for v in parts], axis=0)
+        out = contract(Side[slot], right.astype(jnp.bfloat16))
+        out = out[:, 0:1] + out[:, 8:9]
+        return jnp.where(
+            column_at == 0, out[0:SX], jnp.where(column_at == 1, out[SX : 2 * SX], 0.0)
+        )
+
+    def block(columns, side):
+        columns[0] = columns[0] + jnp.where(w == 0, side, 0.0)
+        columns[2] = columns[2] + jnp.where(w == NW - 1, side, 0.0)
+        return jnp.concatenate(columns, axis=1)
+
+    none = jnp.zeros((SX, 3 * SY), f32)
+    if NS == 2:
+        sign = row_side(None)
+        own, other = band_sum(0), band_sum(sign)
+        ahead, behind = exists(1, 0), exists(-1, 0)
+        bands_summed = [
+            [
+                stream_sum(own[kind], (other[kind], ahead), (other[kind], behind))
+                for kind in range(2)
+            ],
+            [
+                stream_sum(other[kind], (own[kind], behind), (own[kind], ahead))
+                for kind in range(2)
+            ],
+        ]
+        offsets = [0, sign]
+    else:
+        found_at = {ds: band_sum(ds) for ds in bands}
+        bands_summed, offsets = [], [0] + others
+        for ds in offsets:
+            bands_summed.append(
+                [
+                    stream_sum(
+                        found_at[ds][kind],
+                        (found_at[ds + 1][kind], exists(ds + 1, 0)) if ds < reach else None,
+                        (found_at[ds - 1][kind], exists(ds - 1, 0)) if ds > -reach else None,
+                    )
+                    for kind in range(2)
+                ]
+            )
+    top, bottom = none, none
+    for n, ds in enumerate(offsets):
+        here = None if n == 0 or NS == 2 else exists(ds, 0)
+        areas = [area_buf[ds + near, kind] for kind in range(2)]
+        beside = side_load(
+            halves(bands_summed[n][1], areas[1], edge if here is None else edge & here), n
+        )
+        main = halves(bands_summed[n][0], areas[0], here)
+        if n == 0:
+            found = main_load(main, Am[...], 0, owners)
+            middle = block([found[c * SX : (c + 1) * SX] for c in range(3)], beside)
             continue
-        here = exists(ds, 0)
-        lhs = []
-        for kind in range(2):
-            even, odd = summed[ds, kind]
-            if ds + 1 <= reach:
-                more = roll(summed[ds + 1, kind][0], jump, 1)
-                odd = odd + jnp.where(
-                    both((la == EX - 1) & (lc == EZ - 1), exists(ds + 1, 0)), more, 0.0
-                )
-            if ds - 1 >= -reach:
-                more = roll(summed[ds - 1, kind][1], -jump, 1)
-                even = even + jnp.where(both((la == 0) & (lc == 0), exists(ds - 1, 0)), more, 0.0)
-            scale = area_buf[ds + near, kind]
-            flux = jnp.concatenate([even * scale, odd * scale], axis=0) * wij
-            valid = edge if kind else None
-            if here is not None:
-                valid = here if valid is None else valid & here
-            if valid is not None:
-                flux = jnp.where(valid, flux, 0.0)
-            high = flux.astype(jnp.bfloat16).astype(f32)
-            for piece_ in (high, flux - high):
-                lhs.append(
-                    Am[ds + near, :, kind * groups * lanes : (kind + 1) * groups * lanes]
-                    * jnp.concatenate(
-                        [
-                            jnp.broadcast_to(piece_[g : g + 1], (owners, lanes))
-                            for g in range(groups)
-                        ],
-                        axis=1,
-                    )
-                )
-        lhs = jnp.concatenate(
-            [
-                jnp.concatenate([lhs[0], lhs[2]], axis=1),
-                jnp.concatenate([lhs[1], lhs[3]], axis=1),
-            ],
-            axis=0,
-        ).astype(jnp.bfloat16)
-        found = lax.dot_general(
-            lhs, Bt[ds + near], (((1,), (1,)), ((), ())), preferred_element_type=f32
-        )
-        found = found[0:owners] + found[owners : 2 * owners]
-        loads_wide.append(
-            jnp.concatenate([found[c * SX : (c + 1) * SX] for c in range(3)], axis=1)
-        )
-    load_wide = jnp.concatenate(loads_wide, axis=0)
+        found = main_load(main, Am_other[n - 1], n, 8)
+        if NS == 2 or ds > 0:
+            rows = block([jnp.where(sub < 2, roll(found, -2 * c, 0), 0.0) for c in range(3)], beside)
+            bottom = jnp.where(ahead, rows, 0.0) if NS == 2 else rows
+        if NS == 2 or ds < 0:
+            rows = block(
+                [jnp.where(sub > 5, roll(found, 6 - 2 * c, 0), 0.0) for c in range(3)], beside
+            )
+            top = jnp.where(behind, rows, 0.0) if NS == 2 else rows
+    load_wide = jnp.concatenate([top, middle, bottom], axis=0)
     load = centre(load_wide)
     z_wide = load_wide * inv_jacobi
     z_mine = centre(z_wide)
@@ -805,8 +885,9 @@
     groups = 64 // EZ
     reach = min(2, NS - 1)
     near = min(1, reach)
+    others = min(NS - 1, 2)
     SX, SY = shell_cond.shape
-    assert lanes == SY and groups == 16 and NP > 2 and NW > 1
+    assert lanes == SY and SX == 8 and groups == 16 and NP > 2 and NW > 1
     ROWS = face_layout((EX, EY, EZ))[2]
     lhs = jnp.asarray(mxu_tables())
     f32 = jnp.float32
@@ -835,8 +916,9 @@
             V((groups, lanes), f32), V((8, lanes), f32), V((8, lanes), f32),
             V((2 * reach + 1, 2, groups, lanes), f32), V((2 * reach + 1, 4, 8, lanes), f32),
             V((2 * near + 1, 2, 8, lanes), f32),
-            V((2 * near + 1, SY, 2 * groups * lanes), jnp.bfloat16),
-            V((2 * near + 1, 3 * SX, 2 * groups * lanes), f32),
+            V((others + 1, SY, groups * lanes), jnp.bfloat16),
+            V((3 * SX, groups * lanes), f32), V((max(others, 1), 8, groups * lanes), f32),
+            V((others + 1, 2 * SX, groups * lanes), jnp.bfloat16),
             V((2 * SX + groups, SY), f32), V((9, 2 * SX + groups, SY), f32),
             V((1, SY), f32), V((N, SY), f32),
             dma((3, len(OFFSETS))), dma((3, len(OFFSETS))),

time: 35.1 us -> 34.5 us (0.983)
  Pallas kernels: 34.3 us -> 33.7 us
    pallas_call x1, Pallas kernels: 33.6 us -> 33 us  [per_device(): pl.pallas_call(functools.partial(kernel, (NS, NP, NW, EX, EY, EZ)), out_s...]
where the time goes in v2:
time: 34.5 us; the launch traced here: 34.4 us
  Pallas kernels  33.7 us (98%)
  between operations  0.64 us (2%)
    pallas_call x1, Pallas kernels, per_device(): pl.pallas_call(functools.partial(kernel, (NS, NP, NW, EX, EY, EZ)), out_s...  33 us
    pallas_call x1, Pallas kernels, per_device(): pl.pallas_call(hand_over, out_shape=tuple((jax.ShapeDtypeStruct(o.shape,...  0.73 us

profile of v2, /device:TPU:0, one launch (start us, length us, event | category | flops | bytes accessed | tf_op | source)
XLA Modules:
  0.0 34.4 jit_solution(13719704729580086959)
XLA Ops:
  0.6 33.0 %shard_map.103 = (f32[8,8,8,128]{3,2,1,0:T(8,128)S(1)}, f32[8,128]{1,0:T(8,128)S(1)}, f32[8,128]{1,0:T(8,128)S(1)}) custom-call(f32[8,8,8,128]{3,2,1,0:T(8,128)} %temp_hbm.1, bf16[3,8,8,8,128]{4,3,2,1,0:T(8,128)(2,1)} %vel_hbm.1, bf16[1024,768]{1,0:T(8,128)(2,1)} %constant.2.clone.lhs_hbm, f32[3,128]{1,0:T(4,128)} %spacing_hbm.1, f32[1,128]{1,0:T(1,128)} %bitcast.1, ...), custom_call_target="tpu_custom_call" | custom-call | tf_op jit(solution)/shard_map/pallas_call | solution.py:898
  33.6 0.7 %shard_map.104 = (f32[8,8,8,128]{3,2,1,0:T(8,128)}, f32[8,128]{1,0:T(8,128)}, f32[8,128]{1,0:T(8,128)}) custom-call(f32[8,8,8,128]{3,2,1,0:T(8,128)S(1)} %get-tuple-element.6.a_ref, f32[8,128]{1,0:T(8,128)S(1)} %get-tuple-element.7.b_ref, f32[8,128]{1,0:T(8,128)S(1)} %get-tuple-element.8.c_ref), custom_call_target="tpu_custom_call" | custom-call | tf_op jit(solution)/shard_map/pallas_call | solution.py:941
